TPU v7x, 32 devices: a whole 2x2x4 slice. The times are simulated.
32 devices in a mesh: groups: 2 (over x), slab: 16 (over z, y, core).
Axes of the slice: x: 2, y: 2, z: 4, core: 2. Of those that a mesh axis runs over, the one named last changes fastest.
Arguments:
- activations: bfloat16 [2048, 65536], P(('groups', 'slab')), parts along dimension 0, may hold values from 0 to 4
- weights: bfloat16 [6, 2, 512, 128, 128], P(None, None, 'slab'), may hold values from -0.5 to 0.5
- biases: float32 [6, 65536], P(None, 'slab'), may hold values from -1 to 0.5
- columns: int32 [6, 512], P(None, 'slab'), may hold values from 0 to 31
Outputs:
- features: bfloat16 [2048, 65536], P(('groups', 'slab')), parts along dimension 0
There are 2 independent parts, one for each index of `groups`. A program takes and returns all parts, laid end to end along the dimension named above; an argument that names none is the same for every part. Nothing has to cross between parts.
Inputs may be any that keep to these rules, and one draw needn't show every extreme that they name: columns name a block within a group of 32 consecutive blocks.
All inputs are finite; a program needn't handle non-finite values.
Results may differ from a plain program's by a relative error of at most 0.0072.
Values may be sent and summed in bfloat16 or wider, within the bound.
No kernel may reach another device: no remote copies, remote signals or barrier semaphores. Data moves between devices by JAX's collectives and lax.ppermute only.
A program may use at most 128 MiB of HBM per device.

v0:
```python
import jax
import jax.numpy as jnp
from jax import lax
from jax.sharding import PartitionSpec as P

ceiling = 4.0


def from_partner(block, axis, bit):
    count = lax.axis_size(axis)
    route = []
    for low in range(count):
        high = low | 1 << bit
        if high != low and high < count:
            route += [(low, high), (high, low)]
    return lax.ppermute(block, axis, route)


def section_bit(section, remote, log_count):
    return (remote - 1 - section) * (log_count - 1) // (remote - 1)


def local(activations, weights, biases, columns):
    slab_count = lax.axis_size("slab")
    log_count = slab_count.bit_length() - 1
    layer_count = weights.shape[0]
    per_device = weights.shape[2]
    block_width = weights.shape[3]
    local_rows = activations.shape[0]
    remote = (layer_count + 1) // 2
    grouped = activations.reshape(local_rows, slab_count, per_device * block_width)
    stride = 1 << section_bit(0, remote, log_count)
    flipped = grouped.reshape(
        local_rows, slab_count // (2 * stride), 2, stride, per_device * block_width
    )
    flipped = flipped[:, :, ::-1].reshape(local_rows, slab_count, per_device * block_width)
    paired = jnp.stack([grouped, flipped], axis=2)
    arrived = lax.all_to_all(paired, "slab", split_axis=1, concat_axis=0, tiled=True)
    current = arrived[:, 0, 0].reshape(-1, per_device, block_width)
    first_cross = arrived[:, 0, 1].reshape(-1, per_device, block_width)
    for layer_index in range(layer_count):
        if layer_index % 2 == 0:
            if layer_index == 0 and first_cross is not None:
                source = first_cross
            else:
                source = from_partner(
                    current, "slab", section_bit(layer_index // 2, remote, log_count)
                )
        else:
            source = current
        crossing = jnp.take(source, columns[layer_index], axis=1)
        summed = jnp.einsum(
            "rkb,kbc->rkc", current, weights[layer_index, 0], preferred_element_type=jnp.float32
        )
        summed = summed + jnp.einsum(
            "rkb,kbc->rkc", crossing, weights[layer_index, 1], preferred_element_type=jnp.float32
        )
        summed = summed + biases[layer_index].reshape(per_device, block_width)
        current = jnp.clip(summed, 0.0, ceiling).astype(jnp.bfloat16)
    flattened = current.reshape(current.shape[0], per_device * block_width)
    return lax.all_to_all(flattened, "slab", split_axis=0, concat_axis=1, tiled=True)


def solution(mesh):
    placed = (
        P(("groups", "slab"), None),
        P(None, None, "slab", None, None),
        P(None, "slab"),
        P(None, "slab"),
    )
    return jax.shard_map(
        local, mesh=mesh, in_specs=placed, out_specs=P(("groups", "slab"), None), check_vma=False
    )
```

profile of v0, /device:TPU:1, one launch (start us, length us, event | category | flops | bytes accessed | tf_op | source)
XLA Modules:
  0.0 1066.5 jit_solution(5412748452448401006)
XLA Ops:
  0.0 12.1 %copy.28 = bf16[8,8,16,4096]{3,2,1,0:T(8,128)(2,1)} copy(bf16[8,8,16,4096]{3,1,2,0:T(8,128)(2,1)} %bitcast.134) | data formatting | bytes 16777216
  19.9 8.0 pad_maximum_fusion
  27.9 21.4 %copy.18 = bf16[64,16,2,4096]{3,0,2,1:T(8,128)(2,1)} copy(bf16[64,16,2,4096]{3,1,0,2:T(8,128)(2,1)S(1)} %pad_maximum_fusion) | data formatting | bytes 33554432 | tf_op jit(solution)/shard_map/stack | solution.py:37
  49.2 8.1 all-to-all-start
  58.6 295.9 %all-to-all-done = bf16[64,16,2,4096]{3,0,2,1:T(8,128)(2,1)} async-done(((bf16[64,16,2,4096]{3,0,2,1:T(8,128)(2,1)}), bf16[64,16,2,4096]{3,0,2,1:T(8,128)(2,1)}, u32[]{:S(2)}, u32[]{:S(2)}) %all-to-all-start) | async-done | bytes 16777248 | tf_op jit(solution)/shard_map/all_to_all | solution.py:38
  354.5 8.3 copy.19
  369.2 12.0 %copy.22 = bf16[1024,1,1,4096]{0,3,2,1:T(8,128)(2,1)} copy(bf16[1024,1,1,4096]{3,0,2,1:T(8,128)(2,1)} %get-tuple-element.18) | data formatting | bytes 16777216 | tf_op jit(solution)/shard_map/slice | solution.py:40
  381.1 11.4 %copy.23 = bf16[1024,32,128]{2,0,1:T(8,128)(2,1)} copy(bf16[1024,32,128]{0,2,1:T(8,128)(2,1)} %bitcast.132) | data formatting | bytes 16777216 | tf_op jit(solution)/shard_map/reshape;squeeze | solution.py:40
  392.5 11.9 %copy.20 = bf16[1024,1,1,4096]{0,3,2,1:T(8,128)(2,1)} copy(bf16[1024,1,1,4096]{3,0,2,1:T(8,128)(2,1)} %get-tuple-element.19) | data formatting | bytes 16777216 | tf_op jit(solution)/shard_map/slice | solution.py:39
  404.4 8.4 gather_fusion
  412.8 11.8 %fusion.58 = f32[32,1024,128]{2,1,0:T(8,128)} fusion(bf16[1024,32,128]{0,2,1:T(8,128)(2,1)} %bitcast.131, bf16[6,2,32,128,128]{4,3,2,1,0:T(8,128)(2,1)} %param.7), kind=kOutput, calls=%fused_computation.60 | convolution fusion | flops 1073741824 | bytes 26214400 | tf_op jit(solution)/shard_map/rkb,kbc->rkc/dot_general | solution.py:52
  424.6 13.5 %fusion.18 = bf16[1024,32,128]{2,0,1:T(8,128)(2,1)} fusion(f32[32,128]{1,0:T(8,128)S(1)} %bitcast.140, f32[32,1024,128]{2,1,0:T(8,128)} %fusion.58, bf16[32,1024,128]{2,1,0:T(8,128)(2,1)} %gather_fusion, pred[32]{0:T(512)(128)(4,1)S(1)} %get-tuple-element.32, bf16[6,2,32,128,128]{4,3,2,1,0:T(8,128)(2,1)} %param.7), kind=kOutput, calls=%fused_computation.32 | convolution fusion | flops 1094713344 | bytes 34619424 | tf_op jit(solution)/shard_map/rkb,kbc->rkc/dot_general | solution.py:55
  438.2 11.7 %fusion.55 = f32[32,1024,128]{2,1,0:T(8,128)} fusion(bf16[1024,32,128]{2,0,1:T(8,128)(2,1)} %fusion.18, bf16[6,2,32,128,128]{4,3,2,1,0:T(8,128)(2,1)} %param.7), kind=kOutput, calls=%fused_computation.57 | convolution fusion | flops 1073741824 | bytes 26214400 | tf_op jit(solution)/shard_map/rkb,kbc->rkc/dot_general | solution.py:52
  449.8 8.4 gather_fusion.1
  458.2 13.7 %fusion.21 = bf16[1024,32,128]{2,0,1:T(8,128)(2,1)} fusion(f32[32,128]{1,0:T(8,128)S(1)} %bitcast.139, f32[32,1024,128]{2,1,0:T(8,128)} %fusion.55, bf16[32,1024,128]{2,1,0:T(8,128)(2,1)} %gather_fusion.1, pred[32]{0:T(512)(128)(4,1)S(1)} %get-tuple-element.30, bf16[6,2,32,128,128]{4,3,2,1,0:T(8,128)(2,1)} %param.7), kind=kOutput, calls=%fused_computation.33 | convolution fusion | flops 1094713344 | bytes 34619424 | tf_op jit(solution)/shard_map/rkb,kbc->rkc/dot_general | solution.py:55
  471.9 22.8 %collective-permute-start = (bf16[1024,32,128]{2,0,1:T(8,128)(2,1)}, bf16[1024,32,128]{2,0,1:T(8,128)(2,1)}, u32[]{:S(2)}, u32[]{:S(2)}) collective-permute-start(bf16[1024,32,128]{2,0,1:T(8,128)(2,1)} %fusion.21), channel_id=1, source_target_pairs={{0,2},{2,0},{1,3},{3,1},{4,6},{6,4},{5,7},{7,5},{8,10},{10,8},{9,1... | collective-permute-start | bytes 25165832 | tf_op jit(solution)/shard_map/ppermute | solution.py:16
  494.7 11.7 %fusion.52 = f32[32,1024,128]{2,1,0:T(8,128)} fusion(bf16[1024,32,128]{2,0,1:T(8,128)(2,1)} %fusion.21, bf16[6,2,32,128,128]{4,3,2,1,0:T(8,128)(2,1)} %param.7), kind=kOutput, calls=%fused_computation.54 | convolution fusion | flops 1073741824 | bytes 26214400 | tf_op jit(solution)/shard_map/rkb,kbc->rkc/dot_general | solution.py:52
  506.4 169.1 %collective-permute-done = bf16[1024,32,128]{2,0,1:T(8,128)(2,1)} collective-permute-done((bf16[1024,32,128]{2,0,1:T(8,128)(2,1)}, bf16[1024,32,128]{2,0,1:T(8,128)(2,1)}, u32[]{:S(2)}, u32[]{:S(2)}) %collective-permute-start) | collective-permute-done | bytes 8388640 | tf_op jit(solution)/shard_map/ppermute | solution.py:16
  675.5 8.6 gather_fusion.2
  684.1 13.5 %fusion.24 = bf16[1024,32,128]{2,0,1:T(8,128)(2,1)} fusion(f32[32,128]{1,0:T(8,128)S(1)} %bitcast.138, f32[32,1024,128]{2,1,0:T(8,128)} %fusion.52, bf16[32,1024,128]{2,1,0:T(8,128)(2,1)} %gather_fusion.2, pred[32]{0:T(512)(128)(4,1)S(1)} %get-tuple-element.28, bf16[6,2,32,128,128]{4,3,2,1,0:T(8,128)(2,1)} %param.7), kind=kOutput, calls=%fused_computation.34 | convolution fusion | flops 1094713344 | bytes 34619424 | tf_op jit(solution)/shard_map/rkb,kbc->rkc/dot_general | solution.py:55
  697.6 11.7 %fusion.49 = f32[32,1024,128]{2,1,0:T(8,128)} fusion(bf16[1024,32,128]{2,0,1:T(8,128)(2,1)} %fusion.24, bf16[6,2,32,128,128]{4,3,2,1,0:T(8,128)(2,1)} %param.7), kind=kOutput, calls=%fused_computation.51 | convolution fusion | flops 1073741824 | bytes 26214400 | tf_op jit(solution)/shard_map/rkb,kbc->rkc/dot_general | solution.py:52
  709.3 8.5 gather_fusion.3
  717.8 13.5 %fusion.27 = bf16[1024,32,128]{2,0,1:T(8,128)(2,1)} fusion(f32[32,128]{1,0:T(8,128)S(1)} %bitcast.137, f32[32,1024,128]{2,1,0:T(8,128)} %fusion.49, bf16[32,1024,128]{2,1,0:T(8,128)(2,1)} %gather_fusion.3, pred[32]{0:T(512)(128)(4,1)S(1)} %get-tuple-element.26, bf16[6,2,32,128,128]{4,3,2,1,0:T(8,128)(2,1)} %param.7), kind=kOutput, calls=%fused_computation.35 | convolution fusion | flops 1094713344 | bytes 34619424 | tf_op jit(solution)/shard_map/rkb,kbc->rkc/dot_general | solution.py:55
  731.7 11.7 %fusion.46 = f32[32,1024,128]{2,1,0:T(8,128)} fusion(bf16[1024,32,128]{2,0,1:T(8,128)(2,1)} %fusion.27, bf16[6,2,32,128,128]{4,3,2,1,0:T(8,128)(2,1)} %param.7), kind=kOutput, calls=%fused_computation.48 | convolution fusion | flops 1073741824 | bytes 26214400 | tf_op jit(solution)/shard_map/rkb,kbc->rkc/dot_general | solution.py:52
  744.8 8.8 gather_fusion.4
  753.6 13.5 %fusion.30 = bf16[1024,32,128]{2,0,1:T(8,128)(2,1)} fusion(f32[32,128]{1,0:T(8,128)S(1)} %bitcast.136, f32[32,1024,128]{2,1,0:T(8,128)} %fusion.46, bf16[32,1024,128]{2,1,0:T(8,128)(2,1)} %gather_fusion.4, pred[32]{0:T(512)(128)(4,1)S(1)} %get-tuple-element.34, bf16[6,2,32,128,128]{4,3,2,1,0:T(8,128)(2,1)} %param.7), kind=kOutput, calls=%fused_computation.36 | convolution fusion | flops 1094713344 | bytes 34619424 | tf_op jit(solution)/shard_map/rkb,kbc->rkc/dot_general | solution.py:55
  767.1 11.7 %fusion.43 = f32[32,1024,128]{2,1,0:T(8,128)} fusion(bf16[1024,32,128]{2,0,1:T(8,128)(2,1)} %fusion.30, bf16[6,2,32,128,128]{4,3,2,1,0:T(8,128)(2,1)} %param.7), kind=kOutput, calls=%fused_computation.45 | convolution fusion | flops 1073741824 | bytes 26214400 | tf_op jit(solution)/shard_map/rkb,kbc->rkc/dot_general | solution.py:52
  778.8 8.6 gather_fusion.5
  787.4 13.7 %fusion.33 = bf16[1024,32,128]{2,0,1:T(8,128)(2,1)} fusion(f32[32,128]{1,0:T(8,128)S(1)} %bitcast.135, f32[32,1024,128]{2,1,0:T(8,128)} %fusion.43, bf16[32,1024,128]{2,1,0:T(8,128)(2,1)} %gather_fusion.5, pred[32]{0:T(512)(128)(4,1)S(1)} %copy-done.3, bf16[6,2,32,128,128]{4,3,2,1,0:T(8,128)(2,1)} %param.7), kind=kOutput, calls=%fused_computation.37 | convolution fusion | flops 1094713344 | bytes 34619424 | tf_op jit(solution)/shard_map/rkb,kbc->rkc/dot_general | solution.py:55
  801.1 12.2 %copy.24 = bf16[1024,32,128]{2,1,0:T(8,128)(2,1)} copy(bf16[1024,32,128]{2,0,1:T(8,128)(2,1)} %fusion.33) | data formatting | bytes 16777216 | tf_op jit(solution)/shard_map/convert_element_type | solution.py:59
  813.3 13.3 %all_to_all.31 = bf16[16,64,4096]{2,1,0:T(8,128)(2,1)} reshape(bf16[1024,32,128]{2,1,0:T(8,128)(2,1)} %copy.24) | data formatting | bytes 16777216 | tf_op jit(solution)/shard_map/all_to_all | solution.py:61
  826.6 231.7 %all_to_all.37 = bf16[16,64,4096]{2,1,0:T(8,128)(2,1)} all-to-all(bf16[16,64,4096]{2,1,0:T(8,128)(2,1)} %all_to_all.31), channel_id=1, replica_groups=mesh['groups'=2,'slab'=16] {'slab'}, dimensions={0} | all-to-all | bytes 16777216 | tf_op jit(solution)/shard_map/all_to_all | solution.py:61
  (18 shorter events, 25.1 us)
Async XLA Ops:
  49.2 8.2 copy-start.2
  49.2 8.7 copy-start
  49.2 305.2 %all-to-all-start = ((bf16[64,16,2,4096]{3,0,2,1:T(8,128)(2,1)}), bf16[64,16,2,4096]{3,0,2,1:T(8,128)(2,1)}, u32[]{:S(2)}, u32[]{:S(2)}) async-start(bf16[64,16,2,4096]{3,0,2,1:T(8,128)(2,1)} %copy.18), calls=%async_computation | async-start | bytes 33554432 | tf_op jit(solution)/shard_map/all_to_all | solution.py:38
  471.9 203.6 %collective-permute-start = (bf16[1024,32,128]{2,0,1:T(8,128)(2,1)}, bf16[1024,32,128]{2,0,1:T(8,128)(2,1)}, u32[]{:S(2)}, u32[]{:S(2)}) collective-permute-start(bf16[1024,32,128]{2,0,1:T(8,128)(2,1)} %fusion.21), channel_id=1, source_target_pairs={{0,2},{2,0},{1,3},{3,1},{4,6},{6,4},{5,7},{7,5},{8,10},{10,8},{9,1... | collective-permute-start | bytes 25165832 | tf_op jit(solution)/shard_map/ppermute | solution.py:16
  731.3 13.5 %collective-permute-start.1 = (bf16[1024,32,128]{2,0,1:T(8,128)(2,1)}, bf16[1024,32,128]{2,0,1:T(8,128)(2,1)}, u32[]{:S(2)}, u32[]{:S(2)}) collective-permute-start(bf16[1024,32,128]{2,0,1:T(8,128)(2,1)} %fusion.27), channel_id=1, source_target_pairs={{0,1},{1,0},{2,3},{3,2},{4,5},{5,4},{6,7},{7,6},{8,9},{9,8},{10,11... | collective-permute-start | bytes 25165832 | tf_op jit(solution)/shard_map/ppermute | solution.py:16
  778.8 8.6 copy-start.1
  778.8 8.6 copy-start.3
where the time goes:
time: 1070 us
  waiting for transfers between devices  466 us (44%)
  blocking collectives  232 us (22%)
  local copies, waits for them, and re-layouts  177 us (17%)
  matrix products  152 us (14%)
  starting transfers between devices  31.4 us (3%)
    all_to_all x1, waiting for transfers between devices, local(): lax.all_to_all(paired, 'slab', split_axis=1, concat_axis=0, tiled=True)  296 us
    all_to_all x1, blocking collectives, local(): lax.all_to_all(flattened, 'slab', split_axis=0, concat_axis=1, tiled=True)  232 us
    ppermute x2, waiting for transfers between devices, from_partner(): return lax.ppermute(block, axis, route)  171 us
    dot_general x6, matrix products, local(): jnp.einsum('rkb,kbc->rkc', crossing, weights[layer_index, 1], preferred_e...  81.4 us
    dot_general x6, matrix products, local(): jnp.einsum('rkb,kbc->rkc', current, weights[layer_index, 0], preferred_el...  70.2 us
    gather x6, local copies, waits for them, and re-layouts, local(): crossing = jnp.take(source, columns[layer_index], axis=1)  51.3 us
    another operation x2, local copies, waits for them, and re-layouts, local(): paired = jnp.stack([grouped, flipped], axis=2)  29.1 us
    ppermute x2, starting transfers between devices, from_partner(): return lax.ppermute(block, axis, route)  23.2 us
  transfers between devices with their start and end apart: 3, of which 3 were waited for; matrix products, arithmetic and copies ran while one was open for 2% of the time, Pallas kernels for 0%

commit v1 on v0

--- a/solution.py
+++ b/solution.py
@@ -4,6 +4,17 @@
 from jax.sharding import PartitionSpec as P
 
 ceiling = 4.0
+
+
+def in_blocks(x, dim, size):
+    before, after = (x.shape[:dim], x.shape[dim + 1 :])
+    return jnp.moveaxis(x.reshape(*before, size, -1, *after), dim, 0)
+
+
+def laid_out(pieces, dim):
+    shape = list(pieces.shape[1:])
+    shape[dim] *= pieces.shape[0]
+    return jnp.moveaxis(pieces, 0, dim).reshape(shape)
 
 
 def from_partner(block, axis, bit):
@@ -35,7 +46,15 @@
     )
     flipped = flipped[:, :, ::-1].reshape(local_rows, slab_count, per_device * block_width)
     paired = jnp.stack([grouped, flipped], axis=2)
-    arrived = lax.all_to_all(paired, "slab", split_axis=1, concat_axis=0, tiled=True)
+    length, index = (lax.axis_size("slab"), lax.axis_index("slab"))
+    blocks = in_blocks(paired, 1, length)
+    result = blocks
+    for step in range(1, length):
+        target, source_2 = ((index + step) % length, (index - step) % length)
+        sent = lax.dynamic_index_in_dim(blocks, target, 0)
+        received = lax.ppermute(sent, "slab", [(i, (i + step) % length) for i in range(length)])
+        result = lax.dynamic_update_slice_in_dim(result, received, source_2, axis=0)
+    arrived = laid_out(result, 0)
     current = arrived[:, 0, 0].reshape(-1, per_device, block_width)
     first_cross = arrived[:, 0, 1].reshape(-1, per_device, block_width)
     for layer_index in range(layer_count):

time: 1070 us -> 1700 us (1.59); the launches traced: 1070 us -> 1680 us
  local copies, waits for them, and re-layouts: 177 us -> 816 us
  waiting for transfers between devices: 466 us -> 172 us
  starting transfers between devices: 31.4 us -> 276 us
  other arithmetic: 8.53 us -> 72.1 us
  blocking collectives: 232 us -> 187 us
    dynamic_update_slice x0 -> x16, local copies, waits for them, and re-layouts: none -> 578 us  [local(): result = lax.dynamic_update_slice_in_dim(result, received, source_2, axis=0)]
    all_to_all x1 -> x0, waiting for transfers between devices: 296 us -> none  [local(): lax.all_to_all(paired, 'slab', split_axis=1, concat_axis=0, tiled=True)]
    ppermute x0 -> x15, starting transfers between devices: none -> 275 us  [local(): lax.ppermute(sent, 'slab', [(i, (i + step) % length) for i in range(lengt...]
    another operation x1 -> x3, other arithmetic: 8 us -> 64.7 us  [local(): paired = jnp.stack([grouped, flipped], axis=2)]
    ppermute x0 -> x15, local copies, waits for them, and re-layouts: none -> 52.7 us  [local(): lax.ppermute(sent, 'slab', [(i, (i + step) % length) for i in range(lengt...]
    all_to_all x1, blocking collectives: 232 us -> 187 us  [local(): lax.all_to_all(flattened, 'slab', split_axis=0, concat_axis=1, tiled=True)]
    unnamed x9 -> x46, local copies, waits for them, and re-layouts: 12.2 us -> 49.1 us
    ppermute x2, starting transfers between devices: 23.2 us -> 1.23 us  [from_partner(): return lax.ppermute(block, axis, route)]
  transfers between devices with their start and end apart: 3 -> 17, of which waited for: 3 -> 2; matrix products, arithmetic and copies ran while one was open for 2% -> 41% of each run, Pallas kernels for 0% -> 0%
where the time goes in v1:
time: 1700 us; the launch traced here: 1680 us
  local copies, waits for them, and re-layouts  816 us (48%)
  starting transfers between devices  276 us (16%)
  blocking collectives  187 us (11%)
  waiting for transfers between devices  172 us (10%)
  matrix products  152 us (9%)
  other arithmetic  72.1 us (4%)
    dynamic_update_slice x16, local copies, waits for them, and re-layouts, local(): result = lax.dynamic_update_slice_in_dim(result, received, source_2, axis=0)  578 us
    ppermute x15, starting transfers between devices, local(): lax.ppermute(sent, 'slab', [(i, (i + step) % length) for i in range(lengt...  275 us
    all_to_all x1, blocking collectives, local(): lax.all_to_all(flattened, 'slab', split_axis=0, concat_axis=1, tiled=True)  187 us
    ppermute x2, waiting for transfers between devices, from_partner(): return lax.ppermute(block, axis, route)  172 us
    dot_general x6, matrix products, local(): jnp.einsum('rkb,kbc->rkc', crossing, weights[layer_index, 1], preferred_e...  81.7 us
    dot_general x6, matrix products, local(): jnp.einsum('rkb,kbc->rkc', current, weights[layer_index, 0], preferred_el...  70.4 us
    another operation x3, other arithmetic, local(): paired = jnp.stack([grouped, flipped], axis=2)  64.7 us
    ppermute x15, local copies, waits for them, and re-layouts, local(): lax.ppermute(sent, 'slab', [(i, (i + step) % length) for i in range(lengt...  52.7 us
  transfers between devices with their start and end apart: 17, of which 2 were waited for; matrix products, arithmetic and copies ran while one was open for 41% of the time, Pallas kernels for 0%

profile of v1, /device:TPU:1, one launch (start us, length us, event | category | flops | bytes accessed | tf_op | source)
XLA Modules:
  0.0 1675.4 jit_solution(3092649973864988160)
XLA Ops:
  19.9 25.5 %fusion.57 = (bf16[64,1,2,4096]{3,1,0,2:T(2,128)(2,1)S(1)}, bf16[64,1,2,4096]{3,1,0,2:T(2,128)(2,1)S(1)}, bf16[64,1,2,4096]{3,1,0,2:T(2,128)(2,1)S(1)}, bf16[64,...) fusion(s32[]{:T(128)S(6)} %select_n.278, ...), kind=kLoop, calls=%fused_computation.89 | loop fusion | flops 12582912 | bytes 23068696 | tf_op jit(solution)/shard_map/stack | solution.py:48
  62.9 26.9 %fusion.56 = (bf16[64,1,2,4096]{3,1,0,2:T(2,128)(2,1)}, bf16[64,1,2,4096]{3,1,0,2:T(2,128)(2,1)}, bf16[64,1,2,4096]{3,1,0,2:T(2,128)(2,1)}, bf16[64,1,2,4096]{3,...) fusion(s32[]{:T(128)S(6)} %select_n.274, bf16[64,16,1,4096]{3,1,0,2:T(8,128)(2,1)} %bitcast.175, ...), kind=kLoop, calls=%fused_computation.88 | loop fusion | flops 12582912 | bytes 23068696 | tf_op jit(solution)/shard_map/stack | solution.py:48
  109.0 16.6 collective-permute-start.8
  125.6 157.2 %collective-permute-start.9 = (bf16[1,64,1,2,4096]{4,1,3,2,0:T(8,128)(2,1)}, bf16[1,64,1,2,4096]{4,1,3,2,0:T(8,128)(2,1)}, u32[]{:S(2)}, u32[]{:S(2)}) collective-permute-start(bf16[1,64,1,2,4096]{4,1,3,2,0:T(8,128)(2,1)} %bitcast.187), channel_id=1, source_target_pairs={{0,10},{1,11},{2,12},{3,13},{4,14},{5,15},{6,0},{7,1},{8,2},{9,3},... | collective-permute-start | bytes 3145736 | tf_op jit(solution)/shard_map/ppermute | solution.py:55
  312.6 16.3 collective-permute-start.10
  329.0 22.0 %collective-permute-start.11 = (bf16[1,64,1,2,4096]{4,1,3,2,0:T(8,128)(2,1)}, bf16[1,64,1,2,4096]{4,1,3,2,0:T(8,128)(2,1)}, u32[]{:S(2)}, u32[]{:S(2)}) collective-permute-start(bf16[1,64,1,2,4096]{4,1,3,2,0:T(8,128)(2,1)} %bitcast.161), channel_id=1, source_target_pairs={{0,12},{1,13},{2,14},{3,15},{4,0},{5,1},{6,2},{7,3},{8,4},{9,5},{1... | collective-permute-start | bytes 3145736 | tf_op jit(solution)/shard_map/ppermute | solution.py:55
  350.9 34.0 %collective-permute-start.12 = (bf16[1,64,1,2,4096]{4,1,3,2,0:T(8,128)(2,1)}, bf16[1,64,1,2,4096]{4,1,3,2,0:T(8,128)(2,1)}, u32[]{:S(2)}, u32[]{:S(2)}) collective-permute-start(bf16[1,64,1,2,4096]{4,1,3,2,0:T(8,128)(2,1)} %bitcast.160), channel_id=1, source_target_pairs={{0,13},{1,14},{2,15},{3,0},{4,1},{5,2},{6,3},{7,4},{8,5},{9,6},{10... | collective-permute-start | bytes 3145736 | tf_op jit(solution)/shard_map/ppermute | solution.py:55
  384.9 18.3 %collective-permute-start.13 = (bf16[1,64,1,2,4096]{4,1,3,2,0:T(8,128)(2,1)}, bf16[1,64,1,2,4096]{4,1,3,2,0:T(8,128)(2,1)}, u32[]{:S(2)}, u32[]{:S(2)}) collective-permute-start(bf16[1,64,1,2,4096]{4,1,3,2,0:T(8,128)(2,1)} %bitcast.159), channel_id=1, source_target_pairs={{0,14},{1,15},{2,0},{3,1},{4,2},{5,3},{6,4},{7,5},{8,6},{9,7},{10,... | collective-permute-start | bytes 3145736 | tf_op jit(solution)/shard_map/ppermute | solution.py:55
  406.9 37.7 %dynamic_update_slice.45 = bf16[16,64,1,2,4096]{4,0,1,3,2:T(8,128)(2,1)} dynamic-update-slice(bf16[16,64,1,2,4096]{4,0,1,3,2:T(8,128)(2,1)} %fusion, bf16[1,64,1,2,4096]{4,0,1,3,2:T(2,128)(2,1)S(1)} %copy.40, s32[]{:T(128)S(6)} %select_n.224, s32[]{:T(128)} %constant.205.clone.1, s32[]{:T(128)} %constant.205.clone.1, s32[]{:T(128)} %constant.205.clone.1, s32[]{:T(128)} %constant.205.clone.1) | dynamic-update-slice | bytes 2097156 | tf_op jit(solution)/shard_map/dynamic_update_slice | solution.py:56
  448.2 37.5 %dynamic_update_slice.46 = bf16[16,64,1,2,4096]{4,0,1,3,2:T(8,128)(2,1)} dynamic-update-slice(bf16[16,64,1,2,4096]{4,0,1,3,2:T(8,128)(2,1)} %dynamic_update_slice.45, bf16[1,64,1,2,4096]{4,0,1,3,2:T(2,128)(2,1)S(1)} %copy.41, s32[]{:T(128)S(6)} %select_n.228, s32[]{:T(128)} %constant.205.clone.1, s32[]{:T(128)} %constant.205.clone.1, s32[]{:T(128)} %constant.205.clone.1, s32[]{:T(128)} %constant.205.clone.1) | dynamic-update-slice | bytes 2097156 | tf_op jit(solution)/shard_map/dynamic_update_slice | solution.py:56
  489.4 37.5 %dynamic_update_slice.47 = bf16[16,64,1,2,4096]{4,0,1,3,2:T(8,128)(2,1)} dynamic-update-slice(bf16[16,64,1,2,4096]{4,0,1,3,2:T(8,128)(2,1)} %dynamic_update_slice.46, bf16[1,64,1,2,4096]{4,0,1,3,2:T(2,128)(2,1)S(1)} %copy.42, s32[]{:T(128)S(6)} %select_n.232, s32[]{:T(128)} %constant.205.clone.1, s32[]{:T(128)} %constant.205.clone.1, s32[]{:T(128)} %constant.205.clone.1, s32[]{:T(128)} %constant.205.clone.1) | dynamic-update-slice | bytes 2097156 | tf_op jit(solution)/shard_map/dynamic_update_slice | solution.py:56
  530.5 37.5 %dynamic_update_slice.48 = bf16[16,64,1,2,4096]{4,0,1,3,2:T(8,128)(2,1)} dynamic-update-slice(bf16[16,64,1,2,4096]{4,0,1,3,2:T(8,128)(2,1)} %dynamic_update_slice.47, bf16[1,64,1,2,4096]{4,0,1,3,2:T(2,128)(2,1)S(1)} %copy.43, s32[]{:T(128)S(6)} %select_n.236, s32[]{:T(128)} %constant.205.clone.1, s32[]{:T(128)} %constant.205.clone.1, s32[]{:T(128)} %constant.205.clone.1, s32[]{:T(128)} %constant.205.clone.1) | dynamic-update-slice | bytes 2097156 | tf_op jit(solution)/shard_map/dynamic_update_slice | solution.py:56
  571.6 37.5 %dynamic_update_slice.49 = bf16[16,64,1,2,4096]{4,0,1,3,2:T(8,128)(2,1)} dynamic-update-slice(bf16[16,64,1,2,4096]{4,0,1,3,2:T(8,128)(2,1)} %dynamic_update_slice.48, bf16[1,64,1,2,4096]{4,0,1,3,2:T(2,128)(2,1)S(1)} %copy.44, s32[]{:T(128)S(6)} %select_n.240, s32[]{:T(128)} %constant.205.clone.1, s32[]{:T(128)} %constant.205.clone.1, s32[]{:T(128)} %constant.205.clone.1, s32[]{:T(128)} %constant.205.clone.1) | dynamic-update-slice | bytes 2097156 | tf_op jit(solution)/shard_map/dynamic_update_slice | solution.py:56
  612.7 37.5 %dynamic_update_slice.50 = bf16[16,64,1,2,4096]{4,0,1,3,2:T(8,128)(2,1)} dynamic-update-slice(bf16[16,64,1,2,4096]{4,0,1,3,2:T(8,128)(2,1)} %dynamic_update_slice.49, bf16[1,64,1,2,4096]{4,0,1,3,2:T(2,128)(2,1)S(1)} %copy.45, s32[]{:T(128)S(6)} %select_n.244, s32[]{:T(128)} %constant.205.clone.1, s32[]{:T(128)} %constant.205.clone.1, s32[]{:T(128)} %constant.205.clone.1, s32[]{:T(128)} %constant.205.clone.1) | dynamic-update-slice | bytes 2097156 | tf_op jit(solution)/shard_map/dynamic_update_slice | solution.py:56
  653.8 37.9 %dynamic_update_slice.51 = bf16[16,64,1,2,4096]{4,0,1,3,2:T(8,128)(2,1)} dynamic-update-slice(bf16[16,64,1,2,4096]{4,0,1,3,2:T(8,128)(2,1)} %dynamic_update_slice.50, bf16[1,64,1,2,4096]{4,0,1,3,2:T(2,128)(2,1)S(1)} %copy.46, s32[]{:T(128)S(6)} %select_n.248, s32[]{:T(128)} %constant.205.clone.1, s32[]{:T(128)} %constant.205.clone.1, s32[]{:T(128)} %constant.205.clone.1, s32[]{:T(128)} %constant.205.clone.1) | dynamic-update-slice | bytes 2097156 | tf_op jit(solution)/shard_map/dynamic_update_slice | solution.py:56
  695.3 37.5 %dynamic_update_slice.52 = bf16[16,64,1,2,4096]{4,0,1,3,2:T(8,128)(2,1)} dynamic-update-slice(bf16[16,64,1,2,4096]{4,0,1,3,2:T(8,128)(2,1)} %dynamic_update_slice.51, bf16[1,64,1,2,4096]{4,0,1,3,2:T(2,128)(2,1)S(1)} %copy.47, s32[]{:T(128)S(6)} %select_n.252, s32[]{:T(128)} %constant.205.clone.1, s32[]{:T(128)} %constant.205.clone.1, s32[]{:T(128)} %constant.205.clone.1, s32[]{:T(128)} %constant.205.clone.1) | dynamic-update-slice | bytes 2097156 | tf_op jit(solution)/shard_map/dynamic_update_slice | solution.py:56
  736.5 37.5 %dynamic_update_slice.53 = bf16[16,64,1,2,4096]{4,0,1,3,2:T(8,128)(2,1)} dynamic-update-slice(bf16[16,64,1,2,4096]{4,0,1,3,2:T(8,128)(2,1)} %dynamic_update_slice.52, bf16[1,64,1,2,4096]{4,0,1,3,2:T(2,128)(2,1)S(1)} %copy.48, s32[]{:T(128)S(6)} %select_n.256, s32[]{:T(128)} %constant.205.clone.1, s32[]{:T(128)} %constant.205.clone.1, s32[]{:T(128)} %constant.205.clone.1, s32[]{:T(128)} %constant.205.clone.1) | dynamic-update-slice | bytes 2097156 | tf_op jit(solution)/shard_map/dynamic_update_slice | solution.py:56
  777.6 37.5 %dynamic_update_slice.54 = bf16[16,64,1,2,4096]{4,0,1,3,2:T(8,128)(2,1)} dynamic-update-slice(bf16[16,64,1,2,4096]{4,0,1,3,2:T(8,128)(2,1)} %dynamic_update_slice.53, bf16[1,64,1,2,4096]{4,0,1,3,2:T(2,128)(2,1)S(1)} %copy.49, s32[]{:T(128)S(6)} %select_n.260, s32[]{:T(128)} %constant.205.clone.1, s32[]{:T(128)} %constant.205.clone.1, s32[]{:T(128)} %constant.205.clone.1, s32[]{:T(128)} %constant.205.clone.1) | dynamic-update-slice | bytes 2097156 | tf_op jit(solution)/shard_map/dynamic_update_slice | solution.py:56
  818.7 37.5 %dynamic_update_slice.55 = bf16[16,64,1,2,4096]{4,0,1,3,2:T(8,128)(2,1)} dynamic-update-slice(bf16[16,64,1,2,4096]{4,0,1,3,2:T(8,128)(2,1)} %dynamic_update_slice.54, bf16[1,64,1,2,4096]{4,0,1,3,2:T(2,128)(2,1)S(1)} %copy.50, s32[]{:T(128)S(6)} %select_n.264, s32[]{:T(128)} %constant.205.clone.1, s32[]{:T(128)} %constant.205.clone.1, s32[]{:T(128)} %constant.205.clone.1, s32[]{:T(128)} %constant.205.clone.1) | dynamic-update-slice | bytes 2097156 | tf_op jit(solution)/shard_map/dynamic_update_slice | solution.py:56
  859.8 37.5 %dynamic_update_slice.56 = bf16[16,64,1,2,4096]{4,0,1,3,2:T(8,128)(2,1)} dynamic-update-slice(bf16[16,64,1,2,4096]{4,0,1,3,2:T(8,128)(2,1)} %dynamic_update_slice.55, bf16[1,64,1,2,4096]{4,0,1,3,2:T(2,128)(2,1)S(1)} %copy.51, s32[]{:T(128)S(6)} %select_n.268, s32[]{:T(128)} %constant.205.clone.1, s32[]{:T(128)} %constant.205.clone.1, s32[]{:T(128)} %constant.205.clone.1, s32[]{:T(128)} %constant.205.clone.1) | dynamic-update-slice | bytes 2097156 | tf_op jit(solution)/shard_map/dynamic_update_slice | solution.py:56
  900.9 37.6 %dynamic_update_slice.57 = bf16[16,64,1,2,4096]{4,0,1,3,2:T(8,128)(2,1)} dynamic-update-slice(bf16[16,64,1,2,4096]{4,0,1,3,2:T(8,128)(2,1)} %dynamic_update_slice.56, bf16[1,64,1,2,4096]{4,0,1,3,2:T(2,128)(2,1)S(1)} %copy.52, s32[]{:T(128)S(6)} %select_n.272, s32[]{:T(128)} %constant.205.clone.1, s32[]{:T(128)} %constant.205.clone.1, s32[]{:T(128)} %constant.205.clone.1, s32[]{:T(128)} %constant.205.clone.1) | dynamic-update-slice | bytes 2097156 | tf_op jit(solution)/shard_map/dynamic_update_slice | solution.py:56
  942.1 37.5 %dynamic_update_slice.58 = bf16[16,64,1,2,4096]{4,0,1,3,2:T(8,128)(2,1)} dynamic-update-slice(bf16[16,64,1,2,4096]{4,0,1,3,2:T(8,128)(2,1)} %dynamic_update_slice.57, bf16[1,64,1,2,4096]{4,0,1,3,2:T(2,128)(2,1)S(1)} %copy.53, s32[]{:T(128)S(6)} %select_n.276, s32[]{:T(128)} %constant.205.clone.1, s32[]{:T(128)} %constant.205.clone.1, s32[]{:T(128)} %constant.205.clone.1, s32[]{:T(128)} %constant.205.clone.1) | dynamic-update-slice | bytes 2097156 | tf_op jit(solution)/shard_map/dynamic_update_slice | solution.py:56
  983.2 37.5 %dynamic_update_slice.59 = bf16[16,64,1,2,4096]{4,0,1,3,2:T(8,128)(2,1)} dynamic-update-slice(bf16[16,64,1,2,4096]{4,0,1,3,2:T(8,128)(2,1)} %dynamic_update_slice.58, bf16[1,64,1,2,4096]{4,0,1,3,2:T(2,128)(2,1)S(1)} %copy.54, s32[]{:T(128)S(6)} %select_n.280, s32[]{:T(128)} %constant.205.clone.1, s32[]{:T(128)} %constant.205.clone.1, s32[]{:T(128)} %constant.205.clone.1, s32[]{:T(128)} %constant.205.clone.1) | dynamic-update-slice | bytes 2097156 | tf_op jit(solution)/shard_map/dynamic_update_slice | solution.py:56
  1020.7 14.7 copy.55
  1098.1 13.7 fusion.19
  1132.0 13.5 fusion.22
  1157.2 170.3 %collective-permute-done.15 = bf16[1024,32,128]{2,0,1:T(8,128)(2,1)} collective-permute-done((bf16[1024,32,128]{2,0,1:T(8,128)(2,1)}, bf16[1024,32,128]{2,0,1:T(8,128)(2,1)}, u32[]{:S(2)}, u32[]{:S(2)}) %collective-permute-start.15) | collective-permute-done | bytes 8388640 | tf_op jit(solution)/shard_map/ppermute | solution.py:27
  1336.1 13.6 fusion.25
  1370.3 13.6 fusion.28
  1406.8 13.6 fusion.31
  1440.7 13.7 fusion.34
  1479.9 187.5 %all_to_all.19 = bf16[16,64,4096]{2,1,0:T(8,128)(2,1)} all-to-all(bf16[16,64,4096]{2,1,0:T(8,128)(2,1)} %all_to_all.14), channel_id=1, replica_groups=mesh['groups'=2,'slab'=16] {'slab'}, dimensions={0} | all-to-all | bytes 16777216 | tf_op jit(solution)/shard_map/all_to_all | solution.py:80
  (117 shorter events, 340.7 us)
Async XLA Ops:
  47.5 58.0 %collective-permute-start = (bf16[1,64,1,2,4096]{4,1,3,2,0:T(8,128)(2,1)}, bf16[1,64,1,2,4096]{4,1,3,2,0:T(8,128)(2,1)S(1)}, u32[]{:S(2)}, u32[]{:S(2)}) collective-permute-start(bf16[1,64,1,2,4096]{4,1,3,2,0:T(8,128)(2,1)} %bitcast.172), channel_id=1, source_target_pairs={{0,1},{1,2},{2,3},{3,4},{4,5},{5,6},{6,7},{7,8},{8,9},{9,10},{10,1... | collective-permute-start | bytes 3145736 | tf_op jit(solution)/shard_map/ppermute | solution.py:55
  52.2 55.0 %collective-permute-start.1 = (bf16[1,64,1,2,4096]{4,1,3,2,0:T(8,128)(2,1)}, bf16[1,64,1,2,4096]{4,1,3,2,0:T(8,128)(2,1)}, u32[]{:S(2)}, u32[]{:S(2)}) collective-permute-start(bf16[1,64,1,2,4096]{4,1,3,2,0:T(8,128)(2,1)} %bitcast.171), channel_id=1, source_target_pairs={{0,2},{1,3},{2,4},{3,5},{4,6},{5,7},{6,8},{7,9},{8,10},{9,11},{10,... | collective-permute-start | bytes 3145736 | tf_op jit(solution)/shard_map/ppermute | solution.py:55
  54.8 54.1 %collective-permute-start.2 = (bf16[1,64,1,2,4096]{4,1,3,2,0:T(8,128)(2,1)}, bf16[1,64,1,2,4096]{4,1,3,2,0:T(8,128)(2,1)}, u32[]{:S(2)}, u32[]{:S(2)}) collective-permute-start(bf16[1,64,1,2,4096]{4,1,3,2,0:T(8,128)(2,1)} %bitcast.170), channel_id=1, source_target_pairs={{0,3},{1,4},{2,5},{3,6},{4,7},{5,8},{6,9},{7,10},{8,11},{9,12},{10... | collective-permute-start | bytes 3145736 | tf_op jit(solution)/shard_map/ppermute | solution.py:55
  57.3 51.7 %collective-permute-start.3 = (bf16[1,64,1,2,4096]{4,1,3,2,0:T(8,128)(2,1)}, bf16[1,64,1,2,4096]{4,1,3,2,0:T(8,128)(2,1)}, u32[]{:S(2)}, u32[]{:S(2)}) collective-permute-start(bf16[1,64,1,2,4096]{4,1,3,2,0:T(8,128)(2,1)} %bitcast.169), channel_id=1, source_target_pairs={{0,4},{1,5},{2,6},{3,7},{4,8},{5,9},{6,10},{7,11},{8,12},{9,13},{1... | collective-permute-start | bytes 3145736 | tf_op jit(solution)/shard_map/ppermute | solution.py:55
  61.8 63.9 %collective-permute-start.4 = (bf16[1,64,1,2,4096]{4,1,3,2,0:T(8,128)(2,1)}, bf16[1,64,1,2,4096]{4,1,3,2,0:T(8,128)(2,1)}, u32[]{:S(2)}, u32[]{:S(2)}) collective-permute-start(bf16[1,64,1,2,4096]{4,1,3,2,0:T(8,128)(2,1)} %bitcast.168), channel_id=1, source_target_pairs={{0,5},{1,6},{2,7},{3,8},{4,9},{5,10},{6,11},{7,12},{8,13},{9,14},{... | collective-permute-start | bytes 3145736 | tf_op jit(solution)/shard_map/ppermute | solution.py:55
  89.8 11.4 copy-start.2
  89.8 13.5 copy-start.1
  105.5 207.2 %collective-permute-start.5 = (bf16[1,64,1,2,4096]{4,1,3,2,0:T(8,128)(2,1)}, bf16[1,64,1,2,4096]{4,1,3,2,0:T(8,128)(2,1)}, u32[]{:S(2)}, u32[]{:S(2)}) collective-permute-start(bf16[1,64,1,2,4096]{4,1,3,2,0:T(8,128)(2,1)} %bitcast.191), channel_id=1, source_target_pairs={{0,6},{1,7},{2,8},{3,9},{4,10},{5,11},{6,12},{7,13},{8,14},{9,15},... | collective-permute-start | bytes 3145736 | tf_op jit(solution)/shard_map/ppermute | solution.py:55
  107.3 221.7 %collective-permute-start.6 = (bf16[1,64,1,2,4096]{4,1,3,2,0:T(8,128)(2,1)}, bf16[1,64,1,2,4096]{4,1,3,2,0:T(8,128)(2,1)}, u32[]{:S(2)}, u32[]{:S(2)}) collective-permute-start(bf16[1,64,1,2,4096]{4,1,3,2,0:T(8,128)(2,1)} %bitcast.190), channel_id=1, source_target_pairs={{0,7},{1,8},{2,9},{3,10},{4,11},{5,12},{6,13},{7,14},{8,15},{9,0},... | collective-permute-start | bytes 3145736 | tf_op jit(solution)/shard_map/ppermute | solution.py:55
  109.0 242.0 %collective-permute-start.7 = (bf16[1,64,1,2,4096]{4,1,3,2,0:T(8,128)(2,1)}, bf16[1,64,1,2,4096]{4,1,3,2,0:T(8,128)(2,1)}, u32[]{:S(2)}, u32[]{:S(2)}) collective-permute-start(bf16[1,64,1,2,4096]{4,1,3,2,0:T(8,128)(2,1)} %bitcast.189), channel_id=1, source_target_pairs={{0,8},{1,9},{2,10},{3,11},{4,12},{5,13},{6,14},{7,15},{8,0},{9,1},... | collective-permute-start | bytes 3145736 | tf_op jit(solution)/shard_map/ppermute | solution.py:55
  109.0 276.0 %collective-permute-start.8 = (bf16[1,64,1,2,4096]{4,1,3,2,0:T(8,128)(2,1)}, bf16[1,64,1,2,4096]{4,1,3,2,0:T(8,128)(2,1)}, u32[]{:S(2)}, u32[]{:S(2)}) collective-permute-start(bf16[1,64,1,2,4096]{4,1,3,2,0:T(8,128)(2,1)} %bitcast.188), channel_id=1, source_target_pairs={{0,9},{1,10},{2,11},{3,12},{4,13},{5,14},{6,15},{7,0},{8,1},{9,2},... | collective-permute-start | bytes 3145736 | tf_op jit(solution)/shard_map/ppermute | solution.py:55
  125.6 180.2 %slice-start.2 = ((s8[8388608]{0:T(1024)(128)(4,1)}), s8[4194304]{0:T(1024)(128)(4,1)S(1)}, s32[]{:S(2)}) async-start(s8[8388608]{0:T(1024)(128)(4,1)} %bitcast.180), calls=%async_computation.3 | async-start | bytes 8388608
  125.6 180.2 %slice-start.3 = ((s8[8388608]{0:T(1024)(128)(4,1)}), s8[4194304]{0:T(1024)(128)(4,1)S(1)}, s32[]{:S(2)}) async-start(s8[8388608]{0:T(1024)(128)(4,1)} %bitcast.180), calls=%async_computation.4 | async-start | bytes 8388608
  125.6 277.6 %collective-permute-start.9 = (bf16[1,64,1,2,4096]{4,1,3,2,0:T(8,128)(2,1)}, bf16[1,64,1,2,4096]{4,1,3,2,0:T(8,128)(2,1)}, u32[]{:S(2)}, u32[]{:S(2)}) collective-permute-start(bf16[1,64,1,2,4096]{4,1,3,2,0:T(8,128)(2,1)} %bitcast.187), channel_id=1, source_target_pairs={{0,10},{1,11},{2,12},{3,13},{4,14},{5,15},{6,0},{7,1},{8,2},{9,3},... | collective-permute-start | bytes 3145736 | tf_op jit(solution)/shard_map/ppermute | solution.py:55
  295.2 6.4 copy-start
  295.2 10.7 slice-start
  299.5 6.4 slice-start.1
  305.9 97.4 %copy-start.6 = (s32[6,32]{1,0:T(8,128)S(1)}, s32[6,32]{1,0:T(8,128)}, u32[]{:S(2)}) copy-start(s32[6,32]{1,0:T(8,128)} %param.9) | copy-start | bytes 2308
  305.9 98.0 %copy-start.3 = (f32[6,4096]{1,0:T(8,128)S(1)}, f32[6,4096]{1,0:T(8,128)}, u32[]{:S(2)}) copy-start(f32[6,4096]{1,0:T(8,128)} %param.8) | copy-start | bytes 294916
  312.6 502.4 %collective-permute-start.10 = (bf16[1,64,1,2,4096]{4,1,3,2,0:T(8,128)(2,1)}, bf16[1,64,1,2,4096]{4,1,3,2,0:T(8,128)(2,1)}, u32[]{:S(2)}, u32[]{:S(2)}) collective-permute-start(bf16[1,64,1,2,4096]{4,1,3,2,0:T(8,128)(2,1)} %bitcast.162), channel_id=1, source_target_pairs={{0,11},{1,12},{2,13},{3,14},{4,15},{5,0},{6,1},{7,2},{8,3},{9,4},{... | collective-permute-start | bytes 3145736 | tf_op jit(solution)/shard_map/ppermute | solution.py:55
  329.0 527.2 %collective-permute-start.11 = (bf16[1,64,1,2,4096]{4,1,3,2,0:T(8,128)(2,1)}, bf16[1,64,1,2,4096]{4,1,3,2,0:T(8,128)(2,1)}, u32[]{:S(2)}, u32[]{:S(2)}) collective-permute-start(bf16[1,64,1,2,4096]{4,1,3,2,0:T(8,128)(2,1)} %bitcast.161), channel_id=1, source_target_pairs={{0,12},{1,13},{2,14},{3,15},{4,0},{5,1},{6,2},{7,3},{8,4},{9,5},{1... | collective-permute-start | bytes 3145736 | tf_op jit(solution)/shard_map/ppermute | solution.py:55
  350.9 546.3 %collective-permute-start.12 = (bf16[1,64,1,2,4096]{4,1,3,2,0:T(8,128)(2,1)}, bf16[1,64,1,2,4096]{4,1,3,2,0:T(8,128)(2,1)}, u32[]{:S(2)}, u32[]{:S(2)}) collective-permute-start(bf16[1,64,1,2,4096]{4,1,3,2,0:T(8,128)(2,1)} %bitcast.160), channel_id=1, source_target_pairs={{0,13},{1,14},{2,15},{3,0},{4,1},{5,2},{6,3},{7,4},{8,5},{9,6},{10... | collective-permute-start | bytes 3145736 | tf_op jit(solution)/shard_map/ppermute | solution.py:55
  384.9 553.6 %collective-permute-start.13 = (bf16[1,64,1,2,4096]{4,1,3,2,0:T(8,128)(2,1)}, bf16[1,64,1,2,4096]{4,1,3,2,0:T(8,128)(2,1)}, u32[]{:S(2)}, u32[]{:S(2)}) collective-permute-start(bf16[1,64,1,2,4096]{4,1,3,2,0:T(8,128)(2,1)} %bitcast.159), channel_id=1, source_target_pairs={{0,14},{1,15},{2,0},{3,1},{4,2},{5,3},{6,4},{7,5},{8,6},{9,7},{10,... | collective-permute-start | bytes 3145736 | tf_op jit(solution)/shard_map/ppermute | solution.py:55
  403.3 576.4 %collective-permute-start.14 = (bf16[1,64,1,2,4096]{4,1,3,2,0:T(8,128)(2,1)}, bf16[1,64,1,2,4096]{4,1,3,2,0:T(8,128)(2,1)}, u32[]{:S(2)}, u32[]{:S(2)}) collective-permute-start(bf16[1,64,1,2,4096]{4,1,3,2,0:T(8,128)(2,1)} %bitcast.158), channel_id=1, source_target_pairs={{0,15},{1,0},{2,1},{3,2},{4,3},{5,4},{6,5},{7,6},{8,7},{9,8},{10,9... | collective-permute-start | bytes 3145736 | tf_op jit(solution)/shard_map/ppermute | solution.py:55
  1145.5 182.0 %collective-permute-start.15 = (bf16[1024,32,128]{2,0,1:T(8,128)(2,1)}, bf16[1024,32,128]{2,0,1:T(8,128)(2,1)}, u32[]{:S(2)}, u32[]{:S(2)}) collective-permute-start(bf16[1024,32,128]{2,0,1:T(8,128)(2,1)} %fusion.22), channel_id=1, source_target_pairs={{0,2},{2,0},{1,3},{3,1},{4,6},{6,4},{5,7},{7,5},{8,10},{10,8},{9,1... | collective-permute-start | bytes 25165832 | tf_op jit(solution)/shard_map/ppermute | solution.py:27
  1370.3 14.8 copy-start.9
  1370.3 14.8 copy-start.10
  1383.9 14.4 collective-permute-start.16
  1398.2 8.6 copy-start.5
  1398.2 8.6 copy-start.8
  1432.1 8.6 copy-start.4
  1432.1 8.6 copy-start.7
